TPU v7x, 32 devices: a whole 2x2x4 slice. The times are simulated.
32 devices in a mesh: layer: 4 (over y, core), latent: 8 (over z, x).
Axes of the slice: x: 2, y: 2, z: 4, core: 2. Of those that a mesh axis runs over, the one named last changes fastest.
Arguments:
- inputs: bfloat16 [4, 128, 4096], P('layer', 'latent'), may hold values from -6 to 6
- targets: bfloat16 [4, 128, 4096], P('layer', 'latent'), may hold values from -6 to 6
- w_enc: bfloat16 [4, 4096, 8192], P('layer', None, 'latent'), may hold values from -0.09375 to 0.09375
- b_enc: float32 [4, 8192], P('layer', 'latent'), may hold values from -3 to 3
- w_dec: bfloat16 [4, 4, 8192, 4096], P('layer', None, 'latent'), may hold values from -0.03125 to 0.03125
- b_dec: float32 [4, 4096], P('layer'), may hold values from -3 to 3
Outputs:
- grad_enc: bfloat16 [4, 4096, 8192], P('layer', None, 'latent')
- grad_benc: float32 [4, 8192], P('layer', 'latent')
- grad_dec: bfloat16 [4, 4, 8192, 4096], P('layer', None, 'latent')
- grad_bdec: float32 [4, 4096], P('layer')
All inputs are finite; a program needn't handle non-finite values.
Results may differ from a plain program's by a relative error of at most 0.0057.
Values may be sent and summed in bfloat16 or wider, within the bound.
A program may use at most 192 MiB of HBM per device.

v0:
```python
import jax
import jax.numpy as jnp
from jax import lax
from jax.sharding import PartitionSpec as P

penalty = 0.5
eps = 1e-06


def local(inputs, targets, w_enc, b_enc, w_dec, b_dec):
    source = lax.axis_index("layer")
    depth = w_dec.shape[1]
    whole = lax.all_gather(inputs[0], "latent", axis=0, tiled=True)
    pre = jnp.dot(whole, w_enc[0], preferred_element_type=jnp.float32) + b_enc[0]
    positive = jnp.maximum(pre, 0.0)
    act = (positive * positive).astype(jnp.bfloat16)
    valid = (jnp.arange(depth, dtype=jnp.int32) >= source).astype(jnp.float32)
    partial_value = (
        jnp.einsum("nk,tkd->tnd", act, w_dec[0], preferred_element_type=jnp.float32)
        * valid[:, None, None]
    )
    spread = lax.psum_scatter(partial_value, "layer", scatter_dimension=0, tiled=True)
    recon = lax.psum_scatter(spread, "latent", scatter_dimension=1, tiled=True)
    error = recon[0] + b_dec[0] - targets[0].astype(jnp.float32)
    grad_bdec = lax.psum(jnp.sum(error, axis=0), "latent")[None, :]
    err_low = error.astype(jnp.bfloat16)[None]
    stacked = lax.all_gather(err_low, "latent", axis=1, tiled=True)
    errors = lax.all_gather(stacked, "layer", axis=0, tiled=True)
    errors = jnp.where(valid[:, None, None] > 0.0, errors, jnp.zeros_like(errors))
    decoders = w_dec[0]
    squares = jnp.sum(jnp.square(decoders.astype(jnp.float32)), axis=2)
    norms = jnp.sqrt(jnp.sum(squares * valid[:, None], axis=0) + eps)
    back = jnp.einsum("tnd,tkd->nk", errors, decoders, preferred_element_type=jnp.float32)
    d_act = back + penalty * norms[None, :]
    d_pre = d_act * 2.0 * positive
    grad_benc = jnp.sum(d_pre, axis=0)[None, :]
    d_low = d_pre.astype(jnp.bfloat16)
    grad_enc = lax.dot_general(
        whole, d_low, (((0,), (0,)), ((), ())), preferred_element_type=jnp.float32
    ).astype(jnp.bfloat16)[None]
    act_total = jnp.sum(act.astype(jnp.float32), axis=0)
    scale = penalty * act_total / norms
    grad_mse = jnp.einsum("nk,tnd->tkd", act, errors, preferred_element_type=jnp.float32)
    shrink = valid[:, None, None] * scale[None, :, None] * decoders.astype(jnp.float32)
    grad_dec = (grad_mse + shrink).astype(jnp.bfloat16)[None]
    return (grad_enc, grad_benc, grad_dec, grad_bdec)


def solution(mesh):
    placed = (
        P("layer", "latent", None),
        P("layer", "latent", None),
        P("layer", None, "latent"),
        P("layer", "latent"),
        P("layer", None, "latent", None),
        P("layer", None),
    )
    return jax.shard_map(
        local,
        mesh=mesh,
        in_specs=placed,
        out_specs=(
            P("layer", None, "latent"),
            P("layer", "latent"),
            P("layer", None, "latent", None),
            P("layer", None),
        ),
        check_vma=False,
    )
```

profile of v0, /device:TPU:0, one launch (start us, length us, event | category | flops | bytes accessed | tf_op | source)
XLA Modules:
  0.0 456.9 jit_solution(2697420618974324879)
XLA Ops:
  7.2 0.0 all-gather.9.cloned.1.call-start
  7.2 0.7 all-gather.9.cloned.1.call-update
  7.9 0.0 reduce-scatter.3.cloned.1.call-start
  8.0 45.2 %all-gather.9.cloned.1.call-done = bf16[1,128,4096]{2,1,0:T(8,128)(2,1)} async-done(((bf16[1,16,4096]{2,1,0:T(8,128)(2,1)}), bf16[1,128,4096]{2,1,0:T(8,128)(2,1)}) %all-gather.9.cloned.1.call-update) | async-done | bytes 1048592 | tf_op jit(solution)/shard_map/all_gather | solution.py:13
  53.1 4.9 %convert_reduce_fusion = (f32[1024]{0:T(1024)S(1)}, f32[128,1024]{1,0:T(8,128)S(1)}) fusion(f32[1024]{0:T(1024)} %bitcast.82, bf16[1,4096,1024]{2,1,0:T(8,128)(2,1)} %param.8, bf16[1,128,4096]{2,1,0:T(8,128)(2,1)} %all-gather.9.cloned.1.call-done), kind=kOutput, calls=%fused_computation.23 | convolution fusion | flops 1074527232 | bytes 9969664 | tf_op jit(solution)/shard_map/dot_general | solution.py:14
  58.0 18.5 %multiply_bitcast_fusion = f32[4,128,4096]{2,1,0:T(8,128)} fusion(f32[4]{0:T(128)S(1)} %compare_convert_fusion, bf16[1,4,1024,4096]{3,2,1,0:T(8,128)(2,1)} %param.10, f32[128,1024]{1,0:T(8,128)S(1)} %get-tuple-element.15), kind=kOutput, calls=%fused_computation.13 | convolution fusion | flops 4297326592 | bytes 42467344 | tf_op jit(solution)/shard_map/nk,tkd->tnd/dot_general | solution.py:19
  76.5 0.0 copy-start.2
  76.5 0.0 copy-start.3
  76.5 0.0 reduce-scatter.3.cloned.1.call-update
  76.6 0.0 reduce-scatter.5.cloned.1.call-start
  76.6 70.2 %reduce-scatter.3.cloned.1.call-done = f32[1,128,4096]{2,1,0:T(8,128)} async-done(((f32[4,128,4096]{2,1,0:T(8,128)}), f32[1,128,4096]{2,1,0:T(8,128)}) %reduce-scatter.3.cloned.1.call-update) | async-done | bytes 2097168 | tf_op jit(solution)/shard_map/reduce_scatter | solution.py:22
  146.9 0.0 reduce-scatter.5.cloned.1.call-update
  146.9 0.0 all-gather.5.cloned.1.call-start
  146.9 72.2 %reduce-scatter.5.cloned.1.call-done = f32[1,16,4096]{2,1,0:T(8,128)} async-done(((f32[1,128,4096]{2,1,0:T(8,128)}), f32[1,16,4096]{2,1,0:T(8,128)}) %reduce-scatter.5.cloned.1.call-update) | async-done | bytes 262160 | tf_op jit(solution)/shard_map/reduce_scatter | solution.py:23
  219.2 0.0 copy-done.2
  219.2 0.0 copy-done.3
  219.2 1.6 fusion.32
  220.8 0.0 all-gather.5.cloned.1.call-update
  220.8 0.0 all-gather.7.cloned.1.call-start
  220.9 40.2 %all-gather.5.cloned.1.call-done = bf16[1,128,4096]{2,1,0:T(8,128)(2,1)} async-done(((bf16[1,16,4096]{2,1,0:T(8,128)(2,1)}), bf16[1,128,4096]{2,1,0:T(8,128)(2,1)}) %all-gather.5.cloned.1.call-update) | async-done | bytes 1048592 | tf_op jit(solution)/shard_map/all_gather | solution.py:27
  261.1 0.0 all-gather.7.cloned.1.call-update
  261.1 40.6 %copy.16 = bf16[1,4,1024,4096]{2,3,1,0:T(8,128)(2,1)} copy(bf16[1,4,1024,4096]{3,2,1,0:T(8,128)(2,1)} %param.10) | data formatting | bytes 67108864 | tf_op args[4]
  301.6 0.0 copy-start.1
  301.7 11.7 %fusion = f32[4,1024]{1,0:T(4,128)S(1)} fusion(bf16[1,4,1024,4096]{2,3,1,0:T(8,128)(2,1)} %copy.16), kind=kLoop, calls=%fused_computation.2 | loop fusion | flops 50327552 | bytes 33570816 | tf_op jit(solution)/shard_map/reduce_sum | solution.py:31
  313.4 0.1 multiply_reduce_fusion
  313.5 0.1 broadcast_multiply_fusion
  313.5 0.0 copy-done.1
  313.5 0.1 fusion.34
  313.6 35.7 %psum.7 = f32[1,4096]{1,0:T(1,128)} all-reduce(f32[1,4096]{1,0:T(1,128)S(1)} %bitcast.81), channel_id=1, replica_groups=mesh['layer'=4,'latent'=8] {'latent'}, use_global_device_ids=true, to_apply=%region_7.8 | all-reduce | flops 4096 | bytes 32768 | tf_op jit(solution)/shard_map/psum | solution.py:25
  349.3 0.0 all-gather.7.cloned.1.call-done
  349.3 25.4 %fusion.7 = bf16[1,4,1024,4096]{2,3,1,0:T(8,128)(2,1)} fusion(bf16[1,4,1024,4096]{2,3,1,0:T(8,128)(2,1)} %copy.16, f32[4,1024]{1,0:T(4,128)S(1)} %broadcast_multiply_fusion, bf16[4,128,4096]{2,1,0:T(8,128)(2,1)} %all-gather.7.cloned.1.call-done, pred[4]{0:T(512)(128)(4,1)S(1)} %broadcast_compare_fusion, f32[128,1024]{1,0:T(8,128)S(1)} %get-tuple-element.15), kind=kOutput, calls=%fused_computation.9 | convolution fusion | flops 4364435456 | bytes 71843840 | tf_op jit(solution)/shard_map/nk,tnd->tkd/dot_general | solution.py:43
  374.7 40.5 %copy.21 = bf16[1,4,1024,4096]{3,2,1,0:T(8,128)(2,1)} copy(bf16[1,4,1024,4096]{2,3,1,0:T(8,128)(2,1)} %fusion.7) | data formatting | bytes 67108864
  415.2 0.0 copy-start
  415.2 17.6 %fusion.40 = (f32[1024]{0:T(1024)}, bf16[128,1024]{1,0:T(8,128)(2,1)S(1)}) fusion(f32[128,1024]{1,0:T(8,128)S(1)} %get-tuple-element.15, f32[1024]{0:T(1024)S(1)} %get-tuple-element.13, bf16[1,4,1024,4096]{3,2,1,0:T(8,128)(2,1)} %param.10, bf16[4,128,4096]{2,1,0:T(8,128)(2,1)} %all-gather.7.cloned.1.call-done, pred[4]{0:T(512)(128)(4,1)S(1)} %broadcast_compare_fusion), kind=kOutput, calls=%fused_computation.42 | convolution fusion | flops 4297718784 | bytes 38543364 | tf_op jit(solution)/shard_map/tnd,tkd->nk/dot_general | solution.py:33
  432.8 0.0 copy-done
  432.8 5.6 %convert_bitcast_fusion = bf16[1,4096,1024]{1,2,0:T(8,128)(2,1)} fusion(bf16[1,128,4096]{2,1,0:T(8,128)(2,1)S(1)} %copy-done, bf16[128,1024]{1,0:T(8,128)(2,1)S(1)} %get-tuple-element.17), kind=kOutput, calls=%fused_computation.12 | convolution fusion | flops 1077936128 | bytes 9699328 | tf_op jit(solution)/shard_map/dot_general | solution.py:38
  438.4 11.9 %copy.20 = bf16[1,4096,1024]{2,1,0:T(8,128)(2,1)} copy(bf16[1,4096,1024]{1,2,0:T(8,128)(2,1)} %convert_bitcast_fusion) | data formatting | bytes 16777216
  (3 shorter events, 0.0 us)
Async XLA Ops:
  7.2 46.0 %all-gather.9.cloned.1.call-start = ((), (), s32[]{:S(2)}) async-start(), calls=%async_computation.6 | async-start | bytes 1179648 | tf_op jit(solution)/shard_map/all_gather | solution.py:13
  7.9 139.0 %reduce-scatter.3.cloned.1.call-start = ((), (), s32[]{:S(2)}) async-start(), calls=%async_computation.2 | async-start | bytes 10485760 | tf_op jit(solution)/shard_map/reduce_scatter | solution.py:22
  76.5 142.6 %copy-start.2 = (bf16[1,16,4096]{2,1,0:T(8,128)(2,1)S(1)}, bf16[1,16,4096]{2,1,0:T(8,128)(2,1)}, u32[]{:S(2)}) copy-start(bf16[1,16,4096]{2,1,0:T(8,128)(2,1)} %param.7) | copy-start | bytes 393220
  76.5 142.6 %copy-start.3 = (f32[1,4096]{1,0:T(1,128)S(1)}, f32[1,4096]{1,0:T(1,128)}, u32[]{:S(2)}) copy-start(f32[1,4096]{1,0:T(1,128)} %param.11) | copy-start | bytes 49156
  76.6 142.6 %reduce-scatter.5.cloned.1.call-start = ((), (), s32[]{:S(2)}) async-start(), calls=%async_computation.3 | async-start | bytes 2359296 | tf_op jit(solution)/shard_map/reduce_scatter | solution.py:23
  146.9 114.2 %all-gather.5.cloned.1.call-start = ((), (), s32[]{:S(2)}) async-start(), calls=%async_computation.4 | async-start | bytes 1179648 | tf_op jit(solution)/shard_map/all_gather | solution.py:27
  220.8 128.5 %all-gather.7.cloned.1.call-start = ((), (), s32[]{:S(2)}) async-start(), calls=%async_computation.5 | async-start | bytes 5242880 | tf_op jit(solution)/shard_map/all_gather | solution.py:28
  301.6 11.9 %copy-start.1 = (f32[1,16,4096]{2,1,0:T(8,128)S(1)}, f32[1,16,4096]{2,1,0:T(8,128)}, u32[]{:S(2)}) copy-start(f32[1,16,4096]{2,1,0:T(8,128)} %reduce-scatter.5.cloned.1.call-done) | copy-start | bytes 786436
  415.2 17.6 %copy-start = (bf16[1,128,4096]{2,1,0:T(8,128)(2,1)S(1)}, bf16[1,128,4096]{2,1,0:T(8,128)(2,1)}, u32[]{:S(2)}) copy-start(bf16[1,128,4096]{2,1,0:T(8,128)(2,1)} %all-gather.9.cloned.1.call-done) | copy-start | bytes 3145732
Sparse Core Ops, SparseCore 0:
  10.1 42.9 all-gather.8
  76.7 70.1 reduce-scatter.2
  150.4 68.7 reduce-scatter.4
  221.7 39.2 all-gather.4
  262.5 33.1 all-gather.6
where the time goes:
time: 459 us; the launch traced here: 457 us
  waiting for transfers between devices  229 us (50%)
  local copies, waits for them, and re-layouts  93 us (20%)
  matrix products  72 us (16%)
  blocking collectives  35.7 us (8%)
  between operations  13.8 us (3%)
  other arithmetic  13.6 us (3%)
    unnamed x11, local copies, waits for them, and re-layouts  93 us
    reduce_scatter x1, waiting for transfers between devices, local(): recon = lax.psum_scatter(spread, 'latent', scatter_dimension=1, tiled=True)  72.2 us
    reduce_scatter x1, waiting for transfers between devices, local(): lax.psum_scatter(partial_value, 'layer', scatter_dimension=0, tiled=True)  70.2 us
    all_gather x1, waiting for transfers between devices, local(): whole = lax.all_gather(inputs[0], 'latent', axis=0, tiled=True)  45.2 us
    all_gather x1, waiting for transfers between devices, local(): stacked = lax.all_gather(err_low, 'latent', axis=1, tiled=True)  40.2 us
    psum x1, blocking collectives, local(): grad_bdec = lax.psum(jnp.sum(error, axis=0), 'latent')[None, :]  35.7 us
    dot_general x1, matrix products, local(): jnp.einsum('nk,tnd->tkd', act, errors, preferred_element_type=jnp.float32)  25.4 us
    dot_general x1, matrix products, local(): jnp.einsum('nk,tkd->tnd', act, w_dec[0], preferred_element_type=jnp.float32)  18.5 us
  transfers between devices with their start and end apart: 5, of which 4 were waited for; matrix products, arithmetic and copies ran while one was open for 11% of the time, Pallas kernels for 0%

commit v1 on v0

--- a/solution.py
+++ b/solution.py
@@ -2,6 +2,7 @@
 import jax.numpy as jnp
 from jax import lax
 from jax.sharding import PartitionSpec as P
+from jax.lax import axis_index, axis_size, ppermute
 
 penalty = 0.5
 eps = 1e-06
@@ -25,7 +26,23 @@
     grad_bdec = lax.psum(jnp.sum(error, axis=0), "latent")[None, :]
     err_low = error.astype(jnp.bfloat16)[None]
     stacked = lax.all_gather(err_low, "latent", axis=1, tiled=True)
-    errors = lax.all_gather(stacked, "layer", axis=0, tiled=True)
+    o_now, right_arr, t_next = (axis_size("layer"), axis_index("layer"), stacked.shape[0])
+    runs = [(h, (h + 1) % o_now) for h in range(o_now)]
+    errors = jnp.zeros((*stacked.shape[:0], o_now * t_next, *stacked.shape[1:]), stacked.dtype)
+    errors = lax.dynamic_update_slice_in_dim(errors, stacked, right_arr * t_next, axis=0)
+    z1 = local_next = stacked
+    inter = o_now // 2
+    seen = [(h, (h - 1) % o_now) for h in range(o_now)]
+    for b in range(1, inter + 1):
+        z1 = ppermute(z1, "layer", runs)
+        errors = lax.dynamic_update_slice_in_dim(
+            errors, z1, (right_arr - b) % o_now * t_next, axis=0
+        )
+        if b < o_now - inter:
+            local_next = ppermute(local_next, "layer", seen)
+            errors = lax.dynamic_update_slice_in_dim(
+                errors, local_next, (right_arr + b) % o_now * t_next, axis=0
+            )
     errors = jnp.where(valid[:, None, None] > 0.0, errors, jnp.zeros_like(errors))
     decoders = w_dec[0]
     squares = jnp.sum(jnp.square(decoders.astype(jnp.float32)), axis=2)

time: 459 us -> 438 us (0.954)
  waiting for transfers between devices: 229 us -> 194 us
  local copies, waits for them, and re-layouts: 93 us -> 105 us
    all_gather x1, waiting for transfers between devices: 40.2 us -> 0.01 us  [local(): stacked = lax.all_gather(err_low, 'latent', axis=1, tiled=True)]
    ppermute x0 -> x3, waiting for transfers between devices: none -> 5.6 us  [the longest x2 5.6 us: local(): z1 = ppermute(z1, 'layer', runs)]
    ppermute x0 -> x3, local copies, waits for them, and re-layouts: none -> 4.84 us  [the longest x2 3.22 us: local(): z1 = ppermute(z1, 'layer', runs)]
    unnamed x11 -> x13, local copies, waits for them, and re-layouts: 93 us -> 93.1 us
  transfers between devices with their start and end apart: 5 -> 7, of which waited for: 4 -> 4; matrix products, arithmetic and copies ran while one was open for 11% -> 14% of each run, Pallas kernels for 0% -> 0%
where the time goes in v1:
time: 438 us; the launch traced here: 436 us
  waiting for transfers between devices  194 us (44%)
  local copies, waits for them, and re-layouts  105 us (24%)
  matrix products  71.2 us (16%)
  blocking collectives  35.4 us (8%)
  between operations  13.9 us (3%)
  other arithmetic  13.6 us (3%)
    unnamed x13, local copies, waits for them, and re-layouts  93.1 us
    reduce_scatter x1, waiting for transfers between devices, local(): recon = lax.psum_scatter(spread, 'latent', scatter_dimension=1, tiled=True)  72.2 us
    reduce_scatter x1, waiting for transfers between devices, local(): lax.psum_scatter(partial_value, 'layer', scatter_dimension=0, tiled=True)  70.2 us
    all_gather x1, waiting for transfers between devices, local(): whole = lax.all_gather(inputs[0], 'latent', axis=0, tiled=True)  45.2 us
    psum x1, blocking collectives, local(): grad_bdec = lax.psum(jnp.sum(error, axis=0), 'latent')[None, :]  35.4 us
    dot_general x1, matrix products, local(): jnp.einsum('nk,tnd->tkd', act, errors, preferred_element_type=jnp.float32)  24.5 us
    dot_general x1, matrix products, local(): jnp.einsum('nk,tkd->tnd', act, w_dec[0], preferred_element_type=jnp.float32)  18.5 us
    dot_general x1, matrix products, local(): jnp.einsum('tnd,tkd->nk', errors, decoders, preferred_element_type=jnp.fl...  17.8 us
  transfers between devices with their start and end apart: 7, of which 4 were waited for; matrix products, arithmetic and copies ran while one was open for 14% of the time, Pallas kernels for 0%

profile of v1, /device:TPU:0, one launch (start us, length us, event | category | flops | bytes accessed | tf_op | source)
XLA Modules:
  0.0 435.6 jit_solution(2208198624674386164)
XLA Ops:
  7.2 0.0 all-gather.6.cloned.1.call-start
  7.2 0.7 all-gather.6.cloned.1.call-update
  7.9 0.0 reduce-scatter.3.cloned.1.call-start
  8.0 45.2 %all-gather.6.cloned.1.call-done = bf16[1,128,4096]{2,1,0:T(8,128)(2,1)} async-done(((bf16[1,16,4096]{2,1,0:T(8,128)(2,1)}), bf16[1,128,4096]{2,1,0:T(8,128)(2,1)}) %all-gather.6.cloned.1.call-update) | async-done | bytes 1048592 | tf_op jit(solution)/shard_map/all_gather | solution.py:14
  53.1 4.9 %convert_reduce_fusion = (f32[1024]{0:T(1024)S(1)}, f32[128,1024]{1,0:T(8,128)S(1)}) fusion(f32[1024]{0:T(1024)} %bitcast.82, bf16[1,4096,1024]{2,1,0:T(8,128)(2,1)} %param.8, bf16[1,128,4096]{2,1,0:T(8,128)(2,1)} %all-gather.6.cloned.1.call-done), kind=kOutput, calls=%fused_computation.23 | convolution fusion | flops 1074527232 | bytes 9969664 | tf_op jit(solution)/shard_map/dot_general | solution.py:15
  58.0 18.5 %multiply_bitcast_fusion = f32[4,128,4096]{2,1,0:T(8,128)} fusion(f32[4]{0:T(128)S(1)} %compare_convert_fusion, bf16[1,4,1024,4096]{3,2,1,0:T(8,128)(2,1)} %param.10, f32[128,1024]{1,0:T(8,128)S(1)} %get-tuple-element.11), kind=kOutput, calls=%fused_computation.13 | convolution fusion | flops 4297326592 | bytes 42467344 | tf_op jit(solution)/shard_map/nk,tkd->tnd/dot_general | solution.py:20
  76.5 0.0 copy-start.3
  76.5 0.0 copy-start.4
  76.5 0.0 reduce-scatter.3.cloned.1.call-update
  76.6 0.0 reduce-scatter.5.cloned.1.call-start
  76.6 70.2 %reduce-scatter.3.cloned.1.call-done = f32[1,128,4096]{2,1,0:T(8,128)} async-done(((f32[4,128,4096]{2,1,0:T(8,128)}), f32[1,128,4096]{2,1,0:T(8,128)}) %reduce-scatter.3.cloned.1.call-update) | async-done | bytes 2097168 | tf_op jit(solution)/shard_map/reduce_scatter | solution.py:23
  146.9 0.0 reduce-scatter.5.cloned.1.call-update
  146.9 0.0 all-gather.4.cloned.1.call-start
  146.9 72.2 %reduce-scatter.5.cloned.1.call-done = f32[1,16,4096]{2,1,0:T(8,128)} async-done(((f32[1,128,4096]{2,1,0:T(8,128)}), f32[1,16,4096]{2,1,0:T(8,128)}) %reduce-scatter.5.cloned.1.call-update) | async-done | bytes 262160 | tf_op jit(solution)/shard_map/reduce_scatter | solution.py:24
  219.2 0.0 copy-done.3
  219.2 0.0 copy-done.4
  219.2 1.6 fusion.32
  220.8 0.0 all-gather.4.cloned.1.call-update
  220.8 40.6 %copy.10 = bf16[1,4,1024,4096]{2,3,1,0:T(8,128)(2,1)} copy(bf16[1,4,1024,4096]{3,2,1,0:T(8,128)(2,1)} %param.10) | data formatting | bytes 67108864 | tf_op args[4]
  261.5 0.0 copy-start.2
  261.5 0.1 collective-permute-start
  261.5 11.8 %fusion = f32[4,1024]{1,0:T(4,128)S(1)} fusion(bf16[1,4,1024,4096]{2,3,1,0:T(8,128)(2,1)} %copy.10), kind=kLoop, calls=%fused_computation.2 | loop fusion | flops 50327552 | bytes 33570816 | tf_op jit(solution)/shard_map/reduce_sum | solution.py:48
  273.4 0.1 multiply_reduce_fusion
  273.4 0.0 copy-done.1
  273.4 1.7 collective-permute-start.1
  275.1 0.1 broadcast_multiply_fusion
  275.2 0.0 copy-done.2
  275.2 0.1 fusion.34
  275.3 35.4 %psum.7 = f32[1,4096]{1,0:T(1,128)} all-reduce(f32[1,4096]{1,0:T(1,128)S(1)} %bitcast.81), channel_id=1, replica_groups=mesh['layer'=4,'latent'=8] {'latent'}, use_global_device_ids=true, to_apply=%region_7.8 | all-reduce | flops 4096 | bytes 32768 | tf_op jit(solution)/shard_map/psum | solution.py:26
  310.7 0.7 copy.12
  311.4 0.0 collective-permute-done
  311.4 0.2 collective-permute-start.2
  311.6 2.6 broadcast.70
  314.2 1.0 constant_dynamic-update-slice_fusion.3
  315.2 1.6 copy.13
  316.8 0.0 collective-permute-done.1
  316.8 1.6 copy.14
  318.5 1.0 constant_dynamic-update-slice_fusion.2
  319.5 1.0 constant_dynamic-update-slice_fusion.1
  320.5 5.6 %collective-permute-done.2 = bf16[1,128,4096]{2,1,0:T(8,128)(2,1)} collective-permute-done((bf16[1,128,4096]{2,1,0:T(8,128)(2,1)}, bf16[1,128,4096]{2,1,0:T(8,128)(2,1)}, u32[]{:S(2)}, u32[]{:S(2)}) %collective-permute-start.2) | collective-permute-done | bytes 1048608 | tf_op jit(solution)/shard_map/ppermute | solution.py:37
  326.1 1.6 copy.15
  327.8 1.0 constant_dynamic-update-slice_fusion
  328.8 24.5 %fusion.7 = bf16[1,4,1024,4096]{2,3,1,0:T(8,128)(2,1)} fusion(bf16[1,4,1024,4096]{2,3,1,0:T(8,128)(2,1)} %copy.10, f32[4,1024]{1,0:T(4,128)S(1)} %broadcast_multiply_fusion, bf16[4,128,4096]{1,2,0:T(8,128)(2,1)} %constant_dynamic-update-slice_fusion, pred[4]{0:T(512)(128)(4,1)S(1)} %broadcast_compare_fusion, f32[128,1024]{1,0:T(8,128)S(1)} %get-tuple-element.11), kind=kOutput, calls=%fused_computation.9 | convolution fusion | flops 4364435456 | bytes 71843840 | tf_op jit(solution)/shard_map/nk,tnd->tkd/dot_general | solution.py:60
  353.3 17.8 %fusion.40 = (f32[1024]{0:T(1024)}, bf16[128,1024]{1,0:T(8,128)(2,1)S(1)}) fusion(f32[128,1024]{1,0:T(8,128)S(1)} %get-tuple-element.11, f32[1024]{0:T(1024)S(1)} %get-tuple-element.9, bf16[1,4,1024,4096]{3,2,1,0:T(8,128)(2,1)} %param.10, bf16[4,128,4096]{1,2,0:T(8,128)(2,1)} %constant_dynamic-update-slice_fusion, pred[4]{0:T(512)(128)(4,1)S(1)} %broadcast_compare_fusion), kind=kOutput, calls=%fused_computation.46 | convolution fusion | flops 4297718784 | bytes 38543364 | tf_op jit(solution)/shard_map/tnd,tkd->nk/dot_general | solution.py:50
  371.0 40.5 %copy.19 = bf16[1,4,1024,4096]{3,2,1,0:T(8,128)(2,1)} copy(bf16[1,4,1024,4096]{2,3,1,0:T(8,128)(2,1)} %fusion.7) | data formatting | bytes 67108864
  411.6 0.0 copy-done
  411.6 5.6 %convert_bitcast_fusion = bf16[1,4096,1024]{1,2,0:T(8,128)(2,1)} fusion(bf16[1,128,4096]{2,1,0:T(8,128)(2,1)S(1)} %copy-done, bf16[128,1024]{1,0:T(8,128)(2,1)S(1)} %get-tuple-element.13), kind=kOutput, calls=%fused_computation.12 | convolution fusion | flops 1077936128 | bytes 9699328 | tf_op jit(solution)/shard_map/dot_general | solution.py:55
  417.2 11.9 %copy.18 = bf16[1,4096,1024]{2,1,0:T(8,128)(2,1)} copy(bf16[1,4096,1024]{1,2,0:T(8,128)(2,1)} %convert_bitcast_fusion) | data formatting | bytes 16777216
  (6 shorter events, 0.0 us)
Async XLA Ops:
  7.2 46.0 %all-gather.6.cloned.1.call-start = ((), (), s32[]{:S(2)}) async-start(), calls=%async_computation.5 | async-start | bytes 1179648 | tf_op jit(solution)/shard_map/all_gather | solution.py:14
  7.9 139.0 %reduce-scatter.3.cloned.1.call-start = ((), (), s32[]{:S(2)}) async-start(), calls=%async_computation.2 | async-start | bytes 10485760 | tf_op jit(solution)/shard_map/reduce_scatter | solution.py:23
  76.5 142.6 %copy-start.3 = (bf16[1,16,4096]{2,1,0:T(8,128)(2,1)S(1)}, bf16[1,16,4096]{2,1,0:T(8,128)(2,1)}, u32[]{:S(2)}) copy-start(bf16[1,16,4096]{2,1,0:T(8,128)(2,1)} %param.7) | copy-start | bytes 393220
  76.5 142.6 %copy-start.4 = (f32[1,4096]{1,0:T(1,128)S(1)}, f32[1,4096]{1,0:T(1,128)}, u32[]{:S(2)}) copy-start(f32[1,4096]{1,0:T(1,128)} %param.11) | copy-start | bytes 49156
  76.6 142.6 %reduce-scatter.5.cloned.1.call-start = ((), (), s32[]{:S(2)}) async-start(), calls=%async_computation.3 | async-start | bytes 2359296 | tf_op jit(solution)/shard_map/reduce_scatter | solution.py:24
  146.9 114.6 %all-gather.4.cloned.1.call-start = ((), (), s32[]{:S(2)}) async-start(), calls=%async_computation.4 | async-start | bytes 1179648 | tf_op jit(solution)/shard_map/all_gather | solution.py:28
  261.5 13.8 %copy-start.2 = (f32[1,16,4096]{2,1,0:T(8,128)S(1)}, f32[1,16,4096]{2,1,0:T(8,128)}, u32[]{:S(2)}) copy-start(f32[1,16,4096]{2,1,0:T(8,128)} %reduce-scatter.5.cloned.1.call-done) | copy-start | bytes 786436
  261.5 12.0 %copy-start.1 = (bf16[1,128,4096]{2,1,0:T(8,128)(2,1)S(1)}, bf16[1,128,4096]{2,1,0:T(8,128)(2,1)}, u32[]{:S(2)}) copy-start(bf16[1,128,4096]{2,1,0:T(8,128)(2,1)} %all-gather.4.cloned.1.call-done) | copy-start | bytes 3145732
  261.5 49.9 %collective-permute-start = (bf16[1,128,4096]{2,1,0:T(8,128)(2,1)}, bf16[1,128,4096]{2,1,0:T(8,128)(2,1)}, u32[]{:S(2)}, u32[]{:S(2)}) collective-permute-start(bf16[1,128,4096]{2,1,0:T(8,128)(2,1)} %all-gather.4.cloned.1.call-done), channel_id=1, source_target_pairs={{0,8},{8,16},{16,24},{24,0},{1,9},{9,17},{17,25},{25,1},{2,10},{10... | collective-permute-start | bytes 3145736 | tf_op jit(solution)/shard_map/ppermute | solution.py:37
  273.4 43.4 %collective-permute-start.1 = (bf16[1,128,4096]{2,1,0:T(8,128)(2,1)S(1)}, bf16[1,128,4096]{2,1,0:T(8,128)(2,1)}, u32[]{:S(2)}, u32[]{:S(2)}) collective-permute-start(bf16[1,128,4096]{2,1,0:T(8,128)(2,1)S(1)} %copy-done.1), channel_id=1, source_target_pairs={{0,24},{8,0},{16,8},{24,16},{1,25},{9,1},{17,9},{25,17},{2,26},{10... | collective-permute-start | bytes 3145736 | tf_op jit(solution)/shard_map/ppermute | solution.py:42
  311.4 14.8 %collective-permute-start.2 = (bf16[1,128,4096]{2,1,0:T(8,128)(2,1)}, bf16[1,128,4096]{2,1,0:T(8,128)(2,1)}, u32[]{:S(2)}, u32[]{:S(2)}) collective-permute-start(bf16[1,128,4096]{2,1,0:T(8,128)(2,1)} %collective-permute-done), channel_id=1, source_target_pairs={{0,8},{8,16},{16,24},{24,0},{1,9},{9,17},{17,25},{25,1},{2,10},{10... | collective-permute-start | bytes 3145736 | tf_op jit(solution)/shard_map/ppermute | solution.py:37
  371.0 40.5 %copy-start = (bf16[1,128,4096]{2,1,0:T(8,128)(2,1)S(1)}, bf16[1,128,4096]{2,1,0:T(8,128)(2,1)}, u32[]{:S(2)}) copy-start(bf16[1,128,4096]{2,1,0:T(8,128)(2,1)} %all-gather.6.cloned.1.call-done) | copy-start | bytes 3145732
Sparse Core Ops, SparseCore 0:
  10.1 42.9 all-gather.5
  76.7 70.1 reduce-scatter.2
  150.4 68.7 reduce-scatter.4
  221.7 39.2 all-gather.3
